TPU v7x, 32 devices: a whole 2x2x4 slice. The times are simulated.
32 devices in a mesh: fsdp: 8 (over z, core), rows: 4 (over y, x).
Axes of the slice: x: 2, y: 2, z: 4, core: 2. Of those that a mesh axis runs over, the one named last changes fastest.
Arguments:
- query_rows: bfloat16 [8, 1024, 1536], P('fsdp', 'rows'), may hold values from -6 to 6
- key_rows: bfloat16 [8, 1024, 1536], P('fsdp', 'rows'), may hold values from -6 to 6
- value_rows: bfloat16 [8, 1024, 1536], P('fsdp', 'rows'), may hold values from -6 to 6
- grad_out: bfloat16 [8, 1024, 3072], P('fsdp', 'rows'), may hold values from -6 to 6
- w_out: bfloat16 [1536, 3072], P('fsdp'), may hold values from -0.15625 to 0.15625
Outputs:
- grad_query: bfloat16 [8, 1024, 1536], P('fsdp', 'rows')
- grad_key: bfloat16 [8, 1024, 1536], P('fsdp', 'rows')
- grad_value: bfloat16 [8, 1024, 1536], P('fsdp', 'rows')
- grad_w_out: float32 [1536, 3072], P('fsdp')
All inputs are finite; a program needn't handle non-finite values.
Results may differ from a plain program's by a relative error of at most 0.02.
Values may be sent and summed in bfloat16 or wider, within the bound.
No kernel may reach another device: no remote copies, remote signals or barrier semaphores. Data moves between devices by JAX's collectives and lax.ppermute only.
A program may use at most 192 MiB of HBM per device.

v0:
```python
import math
import jax
import jax.numpy as jnp
from jax import lax
from jax.sharding import PartitionSpec as P

HDIM = 128
HEADS = 12
HW = 1536


def split_heads(array, count, groups):
    per_group = HEADS // groups
    return jnp.moveaxis(array.reshape(count, groups, per_group, HDIM), 1, 0)


def join_heads(array, count):
    return jnp.moveaxis(array, 0, 1).reshape(count, HW)


def local(query_rows, key_rows, value_rows, grad_out, w_out):
    tokens = query_rows.shape[1]
    factor = 1.0 / math.sqrt(HDIM)
    grad_flat = grad_out[0]
    groups = HEADS // 4
    grad_attn = lax.dot_general(
        grad_flat,
        lax.all_gather(w_out, "fsdp", axis=0, tiled=True),
        (((1,), (1,)), ((), ())),
        preferred_element_type=jnp.float32,
    ).astype(jnp.bfloat16)
    all_keys, all_values = (
        lax.all_gather(key_rows, "rows", axis=1, tiled=True),
        lax.all_gather(value_rows, "rows", axis=1, tiled=True),
    )
    length = all_keys.shape[1]

    def attend(inputs):
        query_heads, key_heads, value_heads, grad_heads = inputs
        scores = (
            jnp.einsum("qhd,khd->hqk", query_heads, key_heads, preferred_element_type=jnp.float32)
            * factor
        )
        probs = jax.nn.softmax(scores, axis=-1)
        probs_low = probs.astype(jnp.bfloat16)
        attended = jnp.einsum(
            "hqk,khd->qhd", probs_low, value_heads, preferred_element_type=jnp.float32
        )
        value_part = jnp.einsum(
            "hqk,qhd->khd", probs_low, grad_heads, preferred_element_type=jnp.float32
        )
        grad_probs = jnp.einsum(
            "qhd,khd->hqk", grad_heads, value_heads, preferred_element_type=jnp.float32
        )
        centre = jnp.sum(probs * grad_probs, axis=-1, keepdims=True)
        grad_scores = (probs * (grad_probs - centre)).astype(jnp.bfloat16)
        grad_query = (
            jnp.einsum("hqk,khd->qhd", grad_scores, key_heads, preferred_element_type=jnp.float32)
            * factor
        )
        key_part = (
            jnp.einsum("hqk,qhd->khd", grad_scores, query_heads, preferred_element_type=jnp.float32)
            * factor
        )
        return (
            attended.astype(jnp.bfloat16),
            grad_query.astype(jnp.bfloat16),
            key_part,
            value_part,
        )

    attended, grad_query, key_part, value_part = lax.map(
        attend,
        (
            split_heads(query_rows[0], tokens, groups),
            split_heads(all_keys[0], length, groups),
            split_heads(all_values[0], length, groups),
            split_heads(grad_attn, tokens, groups),
        ),
    )
    attended = join_heads(attended, tokens)
    grad_query = join_heads(grad_query, tokens).reshape(1, tokens, HW)
    key_part = join_heads(key_part, length)
    value_part = join_heads(value_part, length)
    grad_key, grad_value = (
        lax.psum_scatter(
            key_part.reshape(1, length, HW).astype(jnp.bfloat16),
            "rows",
            scatter_dimension=1,
            tiled=True,
        ).astype(jnp.float32),
        lax.psum_scatter(
            value_part.reshape(1, length, HW).astype(jnp.bfloat16),
            "rows",
            scatter_dimension=1,
            tiled=True,
        ).astype(jnp.float32),
    )
    term = lax.dot_general(
        attended, grad_flat, (((0,), (0,)), ((), ())), preferred_element_type=jnp.float32
    )
    partial_grad = lax.psum_scatter(
        lax.optimization_barrier(term.astype(jnp.bfloat16))
        .astype(jnp.float32)
        .astype(jnp.bfloat16),
        "fsdp",
        scatter_dimension=0,
        tiled=True,
    )
    grad_w_out = lax.psum(partial_grad, "rows").astype(jnp.float32)
    return (grad_query, grad_key.astype(jnp.bfloat16), grad_value.astype(jnp.bfloat16), grad_w_out)


def solution(mesh):
    in_specs = (
        P("fsdp", "rows", None),
        P("fsdp", "rows", None),
        P("fsdp", "rows", None),
        P("fsdp", "rows", None),
        P("fsdp", None),
    )
    out_specs = (
        P("fsdp", "rows", None),
        P("fsdp", "rows", None),
        P("fsdp", "rows", None),
        P("fsdp", None),
    )
    return jax.shard_map(local, mesh=mesh, in_specs=in_specs, out_specs=out_specs, check_vma=False)
```

profile of v0, /device:TPU:0, one launch (start us, length us, event | category | flops | bytes accessed | tf_op | source)
XLA Modules:
  0.0 541.0 jit_solution(524409484215932579)
XLA Ops:
  11.4 45.0 %all-gather.4.cloned.1.call-done = bf16[1,1024,1536]{2,1,0:T(8,128)(2,1)} async-done(((bf16[1,256,1536]{2,1,0:T(8,128)(2,1)}), bf16[1,1024,1536]{2,1,0:T(8,128)(2,1)}) %all-gather.4.cloned.1.call-update) | async-done | bytes 3145744 | tf_op jit(solution)/shard_map/all_gather | solution.py:34
  56.4 4.7 copy.22
  61.2 87.7 %all-gather.8.cloned.1.call-done = bf16[1536,3072]{1,0:T(8,128)(2,1)} async-done(((bf16[192,3072]{1,0:T(8,128)(2,1)}), bf16[1536,3072]{1,0:T(8,128)(2,1)}) %all-gather.8.cloned.1.call-update) | async-done | bytes 9437200 | tf_op jit(solution)/shard_map/all_gather | solution.py:28
  148.8 7.2 %convolution_convert_fusion.2 = bf16[256,1536]{1,0:T(8,128)(2,1)} fusion(bf16[1536,3072]{1,0:T(8,128)(2,1)} %all-gather.8.cloned.1.call-done, bf16[1,256,3072]{2,1,0:T(8,128)(2,1)S(1)} %copy-done), kind=kOutput, calls=%fused_computation.45 | convolution fusion | flops 2416312320 | bytes 11796480 | tf_op jit(solution)/shard_map/dot_general | solution.py:26
  158.8 34.6 %all-gather.6.cloned.1.call-done = bf16[1,1024,1536]{1,2,0:T(8,128)(2,1)} async-done(((bf16[1,256,1536]{1,2,0:T(8,128)(2,1)}), bf16[1,1024,1536]{1,2,0:T(8,128)(2,1)}) %all-gather.6.cloned.1.call-update) | async-done | bytes 3145744 | tf_op jit(solution)/shard_map/all_gather | solution.py:33
  193.4 84.2 %while.16 = (s32[]{:T(128)}, bf16[3,256,4,128]{1,3,2,0:T(8,128)(2,1)}, bf16[3,256,4,128]{1,3,2,0:T(8,128)(2,1)}, bf16[3,1024,4,128]{1,3,2,0:T(8,128)(2,1)}, bf16...) while((s32[]{:T(128)}, ...), condition=%wide.region_4.5_spmd, body=%wide.region_0.4_spmd.sunk | while | flops 1633554432 | bytes 124291328 | solution.py:72
  195.4 3.2 fusion.81
  198.5 6.7 %fusion.82 = bf16[3,256,4,128]{1,3,2,0:T(8,128)(2,1)} fusion(bf16[3,256,4,128]{1,3,2,0:T(8,128)(2,1)} %get-tuple-element.163, s32[]{:T(128)S(6)} %copy.51, bf16[3,1024,4,128]{1,3,2,0:T(8,128)(2,1)} %get-tuple-element.177, f32[4,256]{1,0:T(4,128)S(1)} %get-tuple-element.148, f32[4,256,1024]{2,1,0:T(8,128)} %copy-done.2), kind=kOutput, calls=%fused_computation.14.clone.1 | convolution fusion | flops 273811456 | bytes 9704448 | tf_op jit(solution)/shard_map/while/body/eval_jaxpr/hqk,khd->qhd/dot_general | solution.py:46
  205.3 6.6 %bitcast_dynamic-update-slice_fusion.5 = bf16[3,1024,4,128]{1,3,2,0:T(8,128)(2,1)} fusion(bf16[3,1024,4,128]{1,3,2,0:T(8,128)(2,1)} %get-tuple-element.166, s32[]{:T(128)S(6)} %copy.51, bf16[3,256,4,128]{3,1,2,0:T(8,128)(2,1)S(1)} %copy-done.6, f32[4,256]{1,0:T(4,128)S(1)} %get-tuple-element.148, f32[4,256,1024]{2,1,0:T(8,128)} %copy-done.2), kind=kOutput, calls=%fused_computation.6.clone.1 | convolution fusion | flops 273680384 | bytes 10753024 | tf_op jit(solution)/shard_map/while/body/eval_jaxpr/hqk,qhd->khd/dot_general | solution.py:49
  211.9 3.4 multiply_reduce_fusion.3
  226.6 6.7 %fusion.82 = bf16[3,256,4,128]{1,3,2,0:T(8,128)(2,1)} fusion(bf16[3,256,4,128]{1,3,2,0:T(8,128)(2,1)} %get-tuple-element.163, s32[]{:T(128)S(6)} %copy.51, bf16[3,1024,4,128]{1,3,2,0:T(8,128)(2,1)} %get-tuple-element.177, f32[4,256]{1,0:T(4,128)S(1)} %get-tuple-element.148, f32[4,256,1024]{2,1,0:T(8,128)} %copy-done.2), kind=kOutput, calls=%fused_computation.14.clone.1 | convolution fusion | flops 273811456 | bytes 9704448 | tf_op jit(solution)/shard_map/while/body/eval_jaxpr/hqk,khd->qhd/dot_general | solution.py:46
  233.4 6.6 %bitcast_dynamic-update-slice_fusion.5 = bf16[3,1024,4,128]{1,3,2,0:T(8,128)(2,1)} fusion(bf16[3,1024,4,128]{1,3,2,0:T(8,128)(2,1)} %get-tuple-element.166, s32[]{:T(128)S(6)} %copy.51, bf16[3,256,4,128]{3,1,2,0:T(8,128)(2,1)S(1)} %copy-done.6, f32[4,256]{1,0:T(4,128)S(1)} %get-tuple-element.148, f32[4,256,1024]{2,1,0:T(8,128)} %copy-done.2), kind=kOutput, calls=%fused_computation.6.clone.1 | convolution fusion | flops 273680384 | bytes 10753024 | tf_op jit(solution)/shard_map/while/body/eval_jaxpr/hqk,qhd->khd/dot_general | solution.py:49
  240.0 3.4 multiply_reduce_fusion.3
  251.5 3.2 fusion.81
  254.7 6.7 %fusion.82 = bf16[3,256,4,128]{1,3,2,0:T(8,128)(2,1)} fusion(bf16[3,256,4,128]{1,3,2,0:T(8,128)(2,1)} %get-tuple-element.163, s32[]{:T(128)S(6)} %copy.51, bf16[3,1024,4,128]{1,3,2,0:T(8,128)(2,1)} %get-tuple-element.177, f32[4,256]{1,0:T(4,128)S(1)} %get-tuple-element.148, f32[4,256,1024]{2,1,0:T(8,128)} %copy-done.2), kind=kOutput, calls=%fused_computation.14.clone.1 | convolution fusion | flops 273811456 | bytes 9704448 | tf_op jit(solution)/shard_map/while/body/eval_jaxpr/hqk,khd->qhd/dot_general | solution.py:46
  261.5 6.6 %bitcast_dynamic-update-slice_fusion.5 = bf16[3,1024,4,128]{1,3,2,0:T(8,128)(2,1)} fusion(bf16[3,1024,4,128]{1,3,2,0:T(8,128)(2,1)} %get-tuple-element.166, s32[]{:T(128)S(6)} %copy.51, bf16[3,256,4,128]{3,1,2,0:T(8,128)(2,1)S(1)} %copy-done.6, f32[4,256]{1,0:T(4,128)S(1)} %get-tuple-element.148, f32[4,256,1024]{2,1,0:T(8,128)} %copy-done.2), kind=kOutput, calls=%fused_computation.6.clone.1 | convolution fusion | flops 273680384 | bytes 10753024 | tf_op jit(solution)/shard_map/while/body/eval_jaxpr/hqk,qhd->khd/dot_general | solution.py:49
  268.0 3.4 multiply_reduce_fusion.3
  277.6 6.2 %convolution_convert_fusion.1 = bf16[1536,3072]{1,0:T(8,128)(2,1)} fusion(bf16[256,1536]{0,1:T(8,128)(2,1)} %bitcast.114, bf16[1,256,3072]{2,1,0:T(8,128)(2,1)S(1)} %copy-done), kind=kOutput, calls=%fused_computation.44 | convolution fusion | flops 2420637696 | bytes 11796480 | tf_op jit(solution)/shard_map/dot_general | solution.py:99
  283.9 99.5 %reduce-scatter.8.cloned.1.call-done = bf16[192,3072]{1,0:T(8,128)(2,1)} async-done(((bf16[1536,3072]{1,0:T(8,128)(2,1)}), bf16[192,3072]{1,0:T(8,128)(2,1)}) %reduce-scatter.8.cloned.1.call-update) | async-done | bytes 1179664 | tf_op jit(solution)/shard_map/reduce_scatter | solution.py:102
  383.6 4.7 copy.37
  388.3 4.7 copy.36
  394.2 45.1 %all-reduce.2.cloned.1.call-done = bf16[192,3072]{1,0:T(8,128)(2,1)} async-done(((bf16[192,3072]{1,0:T(8,128)(2,1)}), bf16[192,3072]{1,0:T(8,128)(2,1)}) %all-reduce.2.cloned.1.call-update) | async-done | bytes 1179664 | tf_op jit(solution)/shard_map/psum | solution.py:110
  442.2 44.4 %reduce-scatter.6.cloned.1.call-done = bf16[1,256,1536]{2,1,0:T(8,128)(2,1)} async-done(((bf16[1,1024,1536]{2,1,0:T(8,128)(2,1)}), bf16[1,256,1536]{2,1,0:T(8,128)(2,1)}) %reduce-scatter.6.cloned.1.call-update) | async-done | bytes 786448 | tf_op jit(solution)/shard_map/reduce_scatter | solution.py:92
  486.6 47.5 %reduce-scatter.4.cloned.1.call-done = bf16[1,256,1536]{2,1,0:T(8,128)(2,1)} async-done(((bf16[1,1024,1536]{2,1,0:T(8,128)(2,1)}), bf16[1,256,1536]{2,1,0:T(8,128)(2,1)}) %reduce-scatter.4.cloned.1.call-update) | async-done | bytes 786448 | tf_op jit(solution)/shard_map/reduce_scatter | solution.py:86
  (73 shorter events, 38.7 us)
Async XLA Ops:
  7.2 141.7 %copy-start = (bf16[1,256,3072]{2,1,0:T(8,128)(2,1)S(1)}, bf16[1,256,3072]{2,1,0:T(8,128)(2,1)}, u32[]{:S(2)}) copy-start(bf16[1,256,3072]{2,1,0:T(8,128)(2,1)} %param.10) | copy-start | bytes 4718596
  7.2 3.9 copy-start.5
  7.2 49.3 %all-gather.4.cloned.1.call-start = ((), (), s32[]{:S(2)}) async-start(), calls=%async_computation.3 | async-start | bytes 3932160 | tf_op jit(solution)/shard_map/all_gather | solution.py:34
  7.9 140.9 %all-gather.8.cloned.1.call-start = ((), (), s32[]{:S(2)}) async-start(), calls=%async_computation.5 | async-start | bytes 10616832 | tf_op jit(solution)/shard_map/all_gather | solution.py:28
  8.7 184.7 %all-gather.6.cloned.1.call-start = ((), (), s32[]{:S(2)}) async-start(), calls=%async_computation.4 | async-start | bytes 3932160 | tf_op jit(solution)/shard_map/all_gather | solution.py:33
  11.0 372.5 %reduce-scatter.8.cloned.1.call-start = ((), (), s32[]{:S(2)}) async-start(), calls=%async_computation.8 | async-start | bytes 10616832 | tf_op jit(solution)/shard_map/reduce_scatter | solution.py:102
  195.4 3.2 copy-start.2
  198.5 6.7 %copy-start.6 = (bf16[3,256,4,128]{3,1,2,0:T(8,128)(2,1)S(1)}, bf16[3,256,4,128]{3,1,2,0:T(8,128)(2,1)}, u32[]{:S(2)}) copy-start(bf16[3,256,4,128]{3,1,2,0:T(8,128)(2,1)} %get-tuple-element.180) | copy-start | bytes 2359300 | tf_op jit(solution)/shard_map/while
  211.9 3.7 copy-start.1
  215.6 3.7 copy-start.3
  219.8 1.7 copy-start.4
  223.4 3.2 copy-start.2
  226.6 6.7 %copy-start.6 = (bf16[3,256,4,128]{3,1,2,0:T(8,128)(2,1)S(1)}, bf16[3,256,4,128]{3,1,2,0:T(8,128)(2,1)}, u32[]{:S(2)}) copy-start(bf16[3,256,4,128]{3,1,2,0:T(8,128)(2,1)} %get-tuple-element.180) | copy-start | bytes 2359300 | tf_op jit(solution)/shard_map/while
  240.0 3.7 copy-start.1
  243.7 3.7 copy-start.3
  247.9 1.7 copy-start.4
  251.5 3.2 copy-start.2
  254.7 6.7 %copy-start.6 = (bf16[3,256,4,128]{3,1,2,0:T(8,128)(2,1)S(1)}, bf16[3,256,4,128]{3,1,2,0:T(8,128)(2,1)}, u32[]{:S(2)}) copy-start(bf16[3,256,4,128]{3,1,2,0:T(8,128)(2,1)} %get-tuple-element.180) | copy-start | bytes 2359300 | tf_op jit(solution)/shard_map/while
  268.0 3.7 copy-start.1
  271.8 3.7 copy-start.3
  283.9 155.4 %all-reduce.2.cloned.1.call-start = ((), (), s32[]{:S(2)}) async-start(), calls=%async_computation.9 | async-start | bytes 2359296 | tf_op jit(solution)/shard_map/psum | solution.py:110
  383.5 103.1 %reduce-scatter.6.cloned.1.call-start = ((), (), s32[]{:S(2)}) async-start(), calls=%async_computation.7 | async-start | bytes 3932160 | tf_op jit(solution)/shard_map/reduce_scatter | solution.py:92
  388.2 145.9 %reduce-scatter.4.cloned.1.call-start = ((), (), s32[]{:S(2)}) async-start(), calls=%async_computation.6 | async-start | bytes 3932160 | tf_op jit(solution)/shard_map/reduce_scatter | solution.py:86
  388.3 4.7 copy-start.7
  (1 other events, 1.7 us)
Sparse Core Ops, SparseCore 0:
  9.8 46.5 all-gather.3
  58.1 90.6 all-gather.7
  151.2 42.1 all-gather.5
  284.0 99.4 reduce-scatter.7
  386.4 52.8 all-reduce.1
  442.7 43.8 reduce-scatter.5
  490.2 43.8 reduce-scatter.3
where the time goes:
time: 542 us; the launch traced here: 541 us
  waiting for transfers between devices  405 us (75%)
  matrix products  80.2 us (15%)
  local copies, waits for them, and re-layouts  26.5 us (5%)
  other arithmetic  14.4 us (3%)
  between operations  14.2 us (3%)
    reduce_scatter x1, waiting for transfers between devices, local(): lax.psum_scatter(lax.optimization_barrier(term.astype(jnp.bfloat16)).asty...  99.5 us
    all_gather x1, waiting for transfers between devices, local(): lax.all_gather(w_out, 'fsdp', axis=0, tiled=True)  87.7 us
    reduce_scatter x1, waiting for transfers between devices, local(): lax.psum_scatter(key_part.reshape(1, length, HW).astype(jnp.bfloat16), 'r...  47.5 us
    psum x1, waiting for transfers between devices, local(): grad_w_out = lax.psum(partial_grad, 'rows').astype(jnp.float32)  45.1 us
    all_gather x1, waiting for transfers between devices, local(): lax.all_gather(value_rows, 'rows', axis=1, tiled=True)  45 us
    reduce_scatter x1, waiting for transfers between devices, local(): lax.psum_scatter(value_part.reshape(1, length, HW).astype(jnp.bfloat16),...  44.4 us
    all_gather x1, waiting for transfers between devices, local(): lax.all_gather(key_rows, 'rows', axis=1, tiled=True)  34.6 us
    dot_general x3, matrix products, attend(): jnp.einsum('hqk,khd->qhd', probs_low, value_heads, preferred_element_type...  20.2 us
  transfers between devices with their start and end apart: 7, of which 7 were waited for; matrix products, arithmetic and copies ran while one was open for 6% of the time, Pallas kernels for 0%

commit v1 on v0

--- a/solution.py
+++ b/solution.py
@@ -7,6 +7,12 @@
 HDIM = 128
 HEADS = 12
 HW = 1536
+
+
+def add_all(value, axis):
+    parts = lax.all_gather(value, axis, axis=0, tiled=False)
+    summed = parts.sum(axis=0)
+    return summed
 
 
 def split_heads(array, count, groups):
@@ -107,7 +113,7 @@
         scatter_dimension=0,
         tiled=True,
     )
-    grad_w_out = lax.psum(partial_grad, "rows").astype(jnp.float32)
+    grad_w_out = add_all(partial_grad, "rows").astype(jnp.float32)
     return (grad_query, grad_key.astype(jnp.bfloat16), grad_value.astype(jnp.bfloat16), grad_w_out)
 
 

time: 542 us -> 543 us (level)
    all_gather x0 -> x1, waiting for transfers between devices: none -> 46.2 us  [add_all(): parts = lax.all_gather(value, axis, axis=0, tiled=False)]
    psum x1 -> x0, waiting for transfers between devices: 45.1 us -> none  [local(): grad_w_out = lax.psum(partial_grad, 'rows').astype(jnp.float32)]
where the time goes in v1:
time: 543 us; the launch traced here: 542 us
  waiting for transfers between devices  404 us (74%)
  matrix products  80.2 us (15%)
  local copies, waits for them, and re-layouts  26.7 us (5%)
  other arithmetic  16.5 us (3%)
  between operations  14.2 us (3%)
    reduce_scatter x1, waiting for transfers between devices, local(): lax.psum_scatter(lax.optimization_barrier(term.astype(jnp.bfloat16)).asty...  99.5 us
    all_gather x1, waiting for transfers between devices, local(): lax.all_gather(w_out, 'fsdp', axis=0, tiled=True)  87.7 us
    reduce_scatter x1, waiting for transfers between devices, local(): lax.psum_scatter(key_part.reshape(1, length, HW).astype(jnp.bfloat16), 'r...  47.5 us
    all_gather x1, waiting for transfers between devices, add_all(): parts = lax.all_gather(value, axis, axis=0, tiled=False)  46.2 us
    all_gather x1, waiting for transfers between devices, local(): lax.all_gather(value_rows, 'rows', axis=1, tiled=True)  45 us
    reduce_scatter x1, waiting for transfers between devices, local(): lax.psum_scatter(value_part.reshape(1, length, HW).astype(jnp.bfloat16),...  42.4 us
    all_gather x1, waiting for transfers between devices, local(): lax.all_gather(key_rows, 'rows', axis=1, tiled=True)  34.6 us
    dot_general x3, matrix products, attend(): jnp.einsum('hqk,khd->qhd', probs_low, value_heads, preferred_element_type...  20.2 us
  transfers between devices with their start and end apart: 7, of which 7 were waited for; matrix products, arithmetic and copies ran while one was open for 6% of the time, Pallas kernels for 0%

profile of v1, /device:TPU:0, one launch (start us, length us, event | category | flops | bytes accessed | tf_op | source)
XLA Modules:
  0.0 542.3 jit_solution(1449971151170399442)
XLA Ops:
  11.4 45.0 %all-gather.6.cloned.1.call-done = bf16[1,1024,1536]{2,1,0:T(8,128)(2,1)} async-done(((bf16[1,256,1536]{2,1,0:T(8,128)(2,1)}), bf16[1,1024,1536]{2,1,0:T(8,128)(2,1)}) %all-gather.6.cloned.1.call-update) | async-done | bytes 3145744 | tf_op jit(solution)/shard_map/all_gather | solution.py:40
  56.4 4.7 copy.22
  61.2 87.7 %all-gather.10.cloned.1.call-done = bf16[1536,3072]{1,0:T(8,128)(2,1)} async-done(((bf16[192,3072]{1,0:T(8,128)(2,1)}), bf16[1536,3072]{1,0:T(8,128)(2,1)}) %all-gather.10.cloned.1.call-update) | async-done | bytes 9437200 | tf_op jit(solution)/shard_map/all_gather | solution.py:34
  148.8 7.2 %convolution_convert_fusion.2 = bf16[256,1536]{1,0:T(8,128)(2,1)} fusion(bf16[1536,3072]{1,0:T(8,128)(2,1)} %all-gather.10.cloned.1.call-done, bf16[1,256,3072]{2,1,0:T(8,128)(2,1)S(1)} %copy-done), kind=kOutput, calls=%fused_computation.45 | convolution fusion | flops 2416312320 | bytes 11796480 | tf_op jit(solution)/shard_map/dot_general | solution.py:32
  158.8 34.6 %all-gather.8.cloned.1.call-done = bf16[1,1024,1536]{1,2,0:T(8,128)(2,1)} async-done(((bf16[1,256,1536]{1,2,0:T(8,128)(2,1)}), bf16[1,1024,1536]{1,2,0:T(8,128)(2,1)}) %all-gather.8.cloned.1.call-update) | async-done | bytes 3145744 | tf_op jit(solution)/shard_map/all_gather | solution.py:39
  193.4 84.2 %while.16 = (s32[]{:T(128)}, bf16[3,256,4,128]{1,3,2,0:T(8,128)(2,1)}, bf16[3,256,4,128]{1,3,2,0:T(8,128)(2,1)}, bf16[3,1024,4,128]{1,3,2,0:T(8,128)(2,1)}, bf16...) while((s32[]{:T(128)}, ...), condition=%wide.region_4.5_spmd, body=%wide.region_0.4_spmd.sunk | while | flops 1633554432 | bytes 124291328 | solution.py:78
  198.5 6.7 %fusion.82 = bf16[3,256,4,128]{1,3,2,0:T(8,128)(2,1)} fusion(bf16[3,256,4,128]{1,3,2,0:T(8,128)(2,1)} %get-tuple-element.163, s32[]{:T(128)S(6)} %copy.51, bf16[3,1024,4,128]{1,3,2,0:T(8,128)(2,1)} %get-tuple-element.177, f32[4,256]{1,0:T(4,128)S(1)} %get-tuple-element.148, f32[4,256,1024]{2,1,0:T(8,128)} %copy-done.2), kind=kOutput, calls=%fused_computation.14.clone.1 | convolution fusion | flops 273811456 | bytes 9704448 | tf_op jit(solution)/shard_map/while/body/eval_jaxpr/hqk,khd->qhd/dot_general | solution.py:52
  205.3 6.6 %bitcast_dynamic-update-slice_fusion.5 = bf16[3,1024,4,128]{1,3,2,0:T(8,128)(2,1)} fusion(bf16[3,1024,4,128]{1,3,2,0:T(8,128)(2,1)} %get-tuple-element.166, s32[]{:T(128)S(6)} %copy.51, bf16[3,256,4,128]{3,1,2,0:T(8,128)(2,1)S(1)} %copy-done.6, f32[4,256]{1,0:T(4,128)S(1)} %get-tuple-element.148, f32[4,256,1024]{2,1,0:T(8,128)} %copy-done.2), kind=kOutput, calls=%fused_computation.6.clone.1 | convolution fusion | flops 273680384 | bytes 10753024 | tf_op jit(solution)/shard_map/while/body/eval_jaxpr/hqk,qhd->khd/dot_general | solution.py:55
  211.9 3.4 multiply_reduce_fusion.3
  226.6 6.7 %fusion.82 = bf16[3,256,4,128]{1,3,2,0:T(8,128)(2,1)} fusion(bf16[3,256,4,128]{1,3,2,0:T(8,128)(2,1)} %get-tuple-element.163, s32[]{:T(128)S(6)} %copy.51, bf16[3,1024,4,128]{1,3,2,0:T(8,128)(2,1)} %get-tuple-element.177, f32[4,256]{1,0:T(4,128)S(1)} %get-tuple-element.148, f32[4,256,1024]{2,1,0:T(8,128)} %copy-done.2), kind=kOutput, calls=%fused_computation.14.clone.1 | convolution fusion | flops 273811456 | bytes 9704448 | tf_op jit(solution)/shard_map/while/body/eval_jaxpr/hqk,khd->qhd/dot_general | solution.py:52
  233.4 6.6 %bitcast_dynamic-update-slice_fusion.5 = bf16[3,1024,4,128]{1,3,2,0:T(8,128)(2,1)} fusion(bf16[3,1024,4,128]{1,3,2,0:T(8,128)(2,1)} %get-tuple-element.166, s32[]{:T(128)S(6)} %copy.51, bf16[3,256,4,128]{3,1,2,0:T(8,128)(2,1)S(1)} %copy-done.6, f32[4,256]{1,0:T(4,128)S(1)} %get-tuple-element.148, f32[4,256,1024]{2,1,0:T(8,128)} %copy-done.2), kind=kOutput, calls=%fused_computation.6.clone.1 | convolution fusion | flops 273680384 | bytes 10753024 | tf_op jit(solution)/shard_map/while/body/eval_jaxpr/hqk,qhd->khd/dot_general | solution.py:55
  240.0 3.4 multiply_reduce_fusion.3
  251.5 3.2 fusion.81
  254.7 6.7 %fusion.82 = bf16[3,256,4,128]{1,3,2,0:T(8,128)(2,1)} fusion(bf16[3,256,4,128]{1,3,2,0:T(8,128)(2,1)} %get-tuple-element.163, s32[]{:T(128)S(6)} %copy.51, bf16[3,1024,4,128]{1,3,2,0:T(8,128)(2,1)} %get-tuple-element.177, f32[4,256]{1,0:T(4,128)S(1)} %get-tuple-element.148, f32[4,256,1024]{2,1,0:T(8,128)} %copy-done.2), kind=kOutput, calls=%fused_computation.14.clone.1 | convolution fusion | flops 273811456 | bytes 9704448 | tf_op jit(solution)/shard_map/while/body/eval_jaxpr/hqk,khd->qhd/dot_general | solution.py:52
  261.5 6.6 %bitcast_dynamic-update-slice_fusion.5 = bf16[3,1024,4,128]{1,3,2,0:T(8,128)(2,1)} fusion(bf16[3,1024,4,128]{1,3,2,0:T(8,128)(2,1)} %get-tuple-element.166, s32[]{:T(128)S(6)} %copy.51, bf16[3,256,4,128]{3,1,2,0:T(8,128)(2,1)S(1)} %copy-done.6, f32[4,256]{1,0:T(4,128)S(1)} %get-tuple-element.148, f32[4,256,1024]{2,1,0:T(8,128)} %copy-done.2), kind=kOutput, calls=%fused_computation.6.clone.1 | convolution fusion | flops 273680384 | bytes 10753024 | tf_op jit(solution)/shard_map/while/body/eval_jaxpr/hqk,qhd->khd/dot_general | solution.py:55
  268.0 3.4 multiply_reduce_fusion.3
  277.6 6.2 %convolution_convert_fusion.1 = bf16[1536,3072]{1,0:T(8,128)(2,1)} fusion(bf16[256,1536]{0,1:T(8,128)(2,1)} %bitcast.116, bf16[1,256,3072]{2,1,0:T(8,128)(2,1)S(1)} %copy-done), kind=kOutput, calls=%fused_computation.44 | convolution fusion | flops 2420637696 | bytes 11796480 | tf_op jit(solution)/shard_map/dot_general | solution.py:105
  283.9 99.5 %reduce-scatter.8.cloned.1.call-done = bf16[192,3072]{1,0:T(8,128)(2,1)} async-done(((bf16[1536,3072]{1,0:T(8,128)(2,1)}), bf16[192,3072]{1,0:T(8,128)(2,1)}) %reduce-scatter.8.cloned.1.call-update) | async-done | bytes 1179664 | tf_op jit(solution)/shard_map/reduce_scatter | solution.py:108
  383.6 4.6 copy.37
  388.3 5.0 copy.36
  394.4 46.2 %all-gather.12.cloned.1.call-done = bf16[768,3072]{1,0:T(8,128)(2,1)} async-done(((bf16[192,3072]{1,0:T(8,128)(2,1)}), bf16[768,3072]{1,0:T(8,128)(2,1)}) %all-gather.12.cloned.1.call-update) | async-done | bytes 4718608 | tf_op jit(solution)/shard_map/all_gather | solution.py:13
  440.6 3.3 reduce_sum.30
  445.6 42.4 %reduce-scatter.6.cloned.1.call-done = bf16[1,256,1536]{2,1,0:T(8,128)(2,1)} async-done(((bf16[1,1024,1536]{2,1,0:T(8,128)(2,1)}), bf16[1,256,1536]{2,1,0:T(8,128)(2,1)}) %reduce-scatter.6.cloned.1.call-update) | async-done | bytes 786448 | tf_op jit(solution)/shard_map/reduce_scatter | solution.py:98
  488.0 47.5 %reduce-scatter.4.cloned.1.call-done = bf16[1,256,1536]{2,1,0:T(8,128)(2,1)} async-done(((bf16[1,1024,1536]{2,1,0:T(8,128)(2,1)}), bf16[1,256,1536]{2,1,0:T(8,128)(2,1)}) %reduce-scatter.4.cloned.1.call-update) | async-done | bytes 786448 | tf_op jit(solution)/shard_map/reduce_scatter | solution.py:92
  (74 shorter events, 40.6 us)
Async XLA Ops:
  7.2 141.7 %copy-start = (bf16[1,256,3072]{2,1,0:T(8,128)(2,1)S(1)}, bf16[1,256,3072]{2,1,0:T(8,128)(2,1)}, u32[]{:S(2)}) copy-start(bf16[1,256,3072]{2,1,0:T(8,128)(2,1)} %param.10) | copy-start | bytes 4718596
  7.2 3.9 copy-start.5
  7.2 49.3 %all-gather.6.cloned.1.call-start = ((), (), s32[]{:S(2)}) async-start(), calls=%async_computation.3 | async-start | bytes 3932160 | tf_op jit(solution)/shard_map/all_gather | solution.py:40
  7.9 140.9 %all-gather.10.cloned.1.call-start = ((), (), s32[]{:S(2)}) async-start(), calls=%async_computation.5 | async-start | bytes 10616832 | tf_op jit(solution)/shard_map/all_gather | solution.py:34
  8.7 184.7 %all-gather.8.cloned.1.call-start = ((), (), s32[]{:S(2)}) async-start(), calls=%async_computation.4 | async-start | bytes 3932160 | tf_op jit(solution)/shard_map/all_gather | solution.py:39
  11.0 372.5 %reduce-scatter.8.cloned.1.call-start = ((), (), s32[]{:S(2)}) async-start(), calls=%async_computation.8 | async-start | bytes 10616832 | tf_op jit(solution)/shard_map/reduce_scatter | solution.py:108
  195.4 3.2 copy-start.2
  198.5 6.7 %copy-start.6 = (bf16[3,256,4,128]{3,1,2,0:T(8,128)(2,1)S(1)}, bf16[3,256,4,128]{3,1,2,0:T(8,128)(2,1)}, u32[]{:S(2)}) copy-start(bf16[3,256,4,128]{3,1,2,0:T(8,128)(2,1)} %get-tuple-element.180) | copy-start | bytes 2359300 | tf_op jit(solution)/shard_map/while
  211.9 3.7 copy-start.1
  215.6 3.7 copy-start.3
  219.8 1.7 copy-start.4
  223.4 3.2 copy-start.2
  226.6 6.7 %copy-start.6 = (bf16[3,256,4,128]{3,1,2,0:T(8,128)(2,1)S(1)}, bf16[3,256,4,128]{3,1,2,0:T(8,128)(2,1)}, u32[]{:S(2)}) copy-start(bf16[3,256,4,128]{3,1,2,0:T(8,128)(2,1)} %get-tuple-element.180) | copy-start | bytes 2359300 | tf_op jit(solution)/shard_map/while
  240.0 3.7 copy-start.1
  243.7 3.7 copy-start.3
  247.9 1.7 copy-start.4
  251.5 3.2 copy-start.2
  254.7 6.7 %copy-start.6 = (bf16[3,256,4,128]{3,1,2,0:T(8,128)(2,1)S(1)}, bf16[3,256,4,128]{3,1,2,0:T(8,128)(2,1)}, u32[]{:S(2)}) copy-start(bf16[3,256,4,128]{3,1,2,0:T(8,128)(2,1)} %get-tuple-element.180) | copy-start | bytes 2359300 | tf_op jit(solution)/shard_map/while
  268.0 3.7 copy-start.1
  271.8 3.7 copy-start.3
  283.9 156.7 %all-gather.12.cloned.1.call-start = ((), (), s32[]{:S(2)}) async-start(), calls=%async_computation.9 | async-start | bytes 5898240 | tf_op jit(solution)/shard_map/all_gather | solution.py:13
  383.5 104.4 %reduce-scatter.6.cloned.1.call-start = ((), (), s32[]{:S(2)}) async-start(), calls=%async_computation.7 | async-start | bytes 3932160 | tf_op jit(solution)/shard_map/reduce_scatter | solution.py:98
  388.2 147.2 %reduce-scatter.4.cloned.1.call-start = ((), (), s32[]{:S(2)}) async-start(), calls=%async_computation.6 | async-start | bytes 3932160 | tf_op jit(solution)/shard_map/reduce_scatter | solution.py:92
  388.3 5.0 copy-start.7
  (1 other events, 1.7 us)
Sparse Core Ops, SparseCore 0:
  9.8 46.5 all-gather.5
  58.1 90.6 all-gather.9
  151.2 42.1 all-gather.7
  284.0 99.4 reduce-scatter.7
  385.2 55.3 all-gather.11
  444.0 43.8 reduce-scatter.5
  491.5 43.8 reduce-scatter.3
